TPU v7x, 32 devices: a whole 2x2x4 slice. The times are simulated.
32 devices in a mesh: orb: 8 (over y, x, core), aux: 4 (over z).
Axes of the slice: x: 2, y: 2, z: 4, core: 2. Of those that a mesh axis runs over, the one named last changes fastest.
Arguments:
- blocks: bfloat16 [32, 256, 6144], P('orb', None, 'aux'), may hold values from -0.65625 to 0.65625
- excitation: float32 [32, 256], replicated, may hold values from 0.5 to 8
- partner: int32 [8, 8], replicated, may hold values from 0 to 3
- neighbours: int32 [8, 8], replicated, may hold values from 0 to 1, as said below
Outputs:
- gradient: bfloat16 [32, 256, 6144], P('orb', None, 'aux')
Inputs may be any that keep to these rules, and one draw needn't show every extreme that they name: neighbours is symmetric: neighbours[d][s] equals neighbours[s][d].
All inputs are finite; a program needn't handle non-finite values.
Results may differ from a plain program's by a relative error of at most 0.0048.
Values may be sent and summed in bfloat16 or wider, within the bound.
No kernel may reach another device: no remote copies, remote signals or barrier semaphores. Data moves between devices by JAX's collectives and lax.ppermute only.
A program may use at most 192 MiB of HBM per device.

v0:
```python
import jax
import jax.numpy as jnp
from jax import lax
from jax.sharding import PartitionSpec as P


def amplitudes(kernel, own_rows, far_rows, weights, excitation):
    denominator = excitation[own_rows][:, :, None] + excitation[far_rows][:, None, :]
    return (-weights[:, None, None] * kernel / denominator).astype(jnp.bfloat16)


def reduce_amplitudes(kernel_part, own_rows, far_rows, weights, excitation):
    kernel = lax.psum(kernel_part, "aux")
    return amplitudes(kernel, own_rows, far_rows, weights, excitation)


def on_device(blocks, excitation, partner, neighbours):
    peers = lax.axis_size("orb")
    anchor = lax.axis_index("orb")
    local_count = blocks.shape[0]
    width = blocks.shape[1]
    aux_width = blocks.shape[2]
    wanted = partner[:, anchor]
    own_rows = anchor * local_count + wanted
    far_rows = jnp.arange(peers, dtype=jnp.int32) * local_count + partner[anchor, :]
    weights = neighbours[anchor, :].astype(jnp.float32)
    outgoing = jnp.take(blocks, wanted, axis=0)
    received = lax.all_to_all(outgoing, "orb", split_axis=0, concat_axis=0, tiled=True)
    kernel_part = jnp.einsum("sap,sbp->sab", outgoing, received, preferred_element_type=jnp.float32)
    amplitude = reduce_amplitudes(kernel_part, own_rows, far_rows, weights, excitation)
    onehot = (wanted[:, None] == jnp.arange(local_count, dtype=jnp.int32)[None, :]).astype(
        jnp.float32
    )
    grouped = 8
    groups = peers // grouped
    amplitude_groups = amplitude.reshape(groups, grouped, width, width)
    received_groups = received.reshape(groups, grouped, width, aux_width)
    onehot_groups = onehot.reshape(groups, grouped, local_count)

    def accumulate(running, pieces):
        product = jnp.einsum(
            "sab,sbp->sap", pieces[0], pieces[1], preferred_element_type=jnp.float32
        )
        added = jnp.einsum("si,sap->iap", pieces[2], product, precision=lax.Precision.HIGHEST)
        return (running + added, None)

    initial = jnp.zeros((local_count, width, aux_width), jnp.float32)
    running, unused = lax.scan(
        accumulate, initial, (amplitude_groups, received_groups, onehot_groups)
    )
    return running.astype(jnp.bfloat16)


def solution(mesh):
    placed = (P("orb", None, "aux"), P(), P(), P())
    return jax.shard_map(
        on_device, mesh=mesh, in_specs=placed, out_specs=P("orb", None, "aux"), check_vma=False
    )
```

profile of v0, /device:TPU:0, one launch (start us, length us, event | category | flops | bytes accessed | tf_op | source)
XLA Modules:
  0.0 209.4 jit_solution(16170676096387874628)
XLA Ops:
  6.5 0.0 copy-start
  6.5 0.0 all-reduce.2.cloned.1.call-start
  6.5 0.9 constant_dynamic-slice_fusion.2
  7.4 0.1 copy.8
  7.5 0.7 fusion.17
  8.2 0.2 copy-done
  8.4 3.6 %gather_fusion = bf16[8,256,1536]{2,1,0:T(8,128)(2,1)} fusion(bf16[4,256,1536]{2,1,0:T(8,128)(2,1)S(1)} %copy-done, s32[1024]{0:T(1024)S(1)} %pad_clamp_fusion.2), kind=kCustom, calls=%fused_computation | custom fusion | bytes 12582944 | tf_op jit(solution)/shard_map/jit(_take)/gather | solution.py:27
  12.0 3.5 %broadcast_select_fusion = bf16[8,256,1536]{2,1,0:T(8,128)(2,1)S(1)} fusion(bf16[8,256,1536]{2,1,0:T(8,128)(2,1)} %gather_fusion, pred[8]{0:T(512)(128)(4,1)S(1)} %and_bitcast_fusion), kind=kLoop, calls=%fused_computation.5 | loop fusion | flops 3145728 | bytes 12582920 | tf_op jit(solution)/shard_map/jit(_take)/select_n | solution.py:27
  15.5 76.5 %all_to_all.5 = bf16[8,256,1536]{2,1,0:T(8,128)(2,1)S(1)} all-to-all(bf16[8,256,1536]{2,1,0:T(8,128)(2,1)S(1)} %broadcast_select_fusion), channel_id=1, replica_groups=mesh['orb'=8,'aux'=4] {'orb'}, dimensions={0} | all-to-all | bytes 12582912 | tf_op jit(solution)/shard_map/all_to_all | solution.py:28
  92.0 0.0 copy-start.1
  92.0 2.6 %copy-done.1 = bf16[8,256,1536]{2,1,0:T(8,128)(2,1)} copy-done((bf16[8,256,1536]{2,1,0:T(8,128)(2,1)}, bf16[8,256,1536]{2,1,0:T(8,128)(2,1)S(1)}, u32[]{:S(2)}) %copy-start.1) | copy-done | bytes 6291480
  94.7 0.0 copy-start.2
  94.7 3.1 %fusion.20 = f32[8,256,256]{2,1,0:T(8,128)} fusion(bf16[8,256,1536]{2,1,0:T(8,128)(2,1)S(1)} %broadcast_select_fusion, bf16[8,256,1536]{2,1,0:T(8,128)(2,1)S(1)} %all_to_all.5), kind=kOutput, calls=%fused_computation.33 | convolution fusion | flops 1610612736 | bytes 14680064 | tf_op jit(solution)/shard_map/sap,sbp->sab/dot_general | solution.py:29
  97.8 0.0 all-reduce.2.cloned.1.call-update
  97.8 0.0 copy-done.2
  97.8 0.6 gather_fusion.1
  98.4 0.6 gather_fusion.2
  99.0 0.7 fusion.14
  99.7 84.2 %all-reduce.2.cloned.1.call-done = f32[8,256,256]{2,1,0:T(8,128)} async-done(((f32[8,256,256]{2,1,0:T(8,128)}), f32[8,256,256]{2,1,0:T(8,128)}) %all-reduce.2.cloned.1.call-update) | async-done | bytes 2097168 | tf_op jit(solution)/shard_map/psum | solution.py:13
  183.9 5.3 %fusion.5 = f32[8,256,1536]{2,1,0:T(8,128)S(1)} fusion(bf16[8,256,1536]{2,1,0:T(8,128)(2,1)} %copy-done.1, f32[8,256,256]{2,1,0:T(8,128)} %all-reduce.2.cloned.1.call-done, f32[8,256]{1,0:T(8,128)S(1)} %gather_fusion.2, f32[8,256]{1,0:T(8,128)S(1)} %gather_fusion.1, f32[8]{0:T(128)S(1)} %fusion.14), kind=kOutput, calls=%fused_computation.8 | convolution fusion | flops 1612709888 | bytes 20987936 | tf_op jit(solution)/shard_map/while/body/eval_jaxpr/sab,sbp->sap/dot_general | solution.py:41
  189.1 11.2 %fusion.2 = bf16[4,256,1536]{2,0,1:T(4,128)(2,1)S(1)} fusion(f32[8,256,1536]{2,1,0:T(8,128)S(1)} %fusion.5, s32[8]{0:T(128)S(1)} %bitcast.25), kind=kOutput, calls=%fused_computation.6 | convolution fusion | flops 152567840 | bytes 15728672 | tf_op jit(solution)/shard_map/while/body/eval_jaxpr/si,sap->iap/dot_general | solution.py:44
  200.3 2.2 %copy.6 = bf16[4,256,1536]{2,1,0:T(8,128)(2,1)} copy(bf16[4,256,1536]{2,0,1:T(4,128)(2,1)S(1)} %fusion.2) | data formatting | bytes 6291456 | tf_op jit(solution)/shard_map/convert_element_type | solution.py:51
  (4 shorter events, 0.0 us)
Async XLA Ops:
  6.5 1.9 copy-start
  6.5 177.3 %all-reduce.2.cloned.1.call-start = ((), (), s32[]{:S(2)}) async-start(), calls=%async_computation.1 | async-start | bytes 4194304 | tf_op jit(solution)/shard_map/psum | solution.py:13
  92.0 2.7 %copy-start.1 = (bf16[8,256,1536]{2,1,0:T(8,128)(2,1)}, bf16[8,256,1536]{2,1,0:T(8,128)(2,1)S(1)}, u32[]{:S(2)}) copy-start(bf16[8,256,1536]{2,1,0:T(8,128)(2,1)S(1)} %all_to_all.5) | copy-start | bytes 18874372
  94.7 3.2 %copy-start.2 = (f32[32,256]{1,0:T(8,128)S(1)}, f32[32,256]{1,0:T(8,128)}, u32[]{:S(2)}) copy-start(f32[32,256]{1,0:T(8,128)} %param.5) | copy-start | bytes 98308
Sparse Core Ops, SparseCore 0:
  97.9 85.8 all-reduce.1
where the time goes:
time: 210 us; the launch traced here: 209 us
  waiting for transfers between devices  84.2 us (40%)
  blocking collectives  76.5 us (36%)
  matrix products  19.6 us (9%)
  between operations  13.4 us (6%)
  local copies, waits for them, and re-layouts  10.8 us (5%)
  other arithmetic  4.87 us (2%)
    psum x1, waiting for transfers between devices, reduce_amplitudes(): kernel = lax.psum(kernel_part, 'aux')  84.2 us
    all_to_all x1, blocking collectives, on_device(): lax.all_to_all(outgoing, 'orb', split_axis=0, concat_axis=0, tiled=True)  76.5 us
    dot_general x1, matrix products, accumulate(): jnp.einsum('si,sap->iap', pieces[2], product, precision=lax.Precision.HIG...  11.2 us
    dot_general x1, matrix products, accumulate(): jnp.einsum('sab,sbp->sap', pieces[0], pieces[1], preferred_element_type=j...  5.28 us
  transfers between devices with their start and end apart: 1, of which 1 were waited for; matrix products, arithmetic and copies ran while one was open for 1% of the time, Pallas kernels for 0%

commit v1 on v0

--- a/solution.py
+++ b/solution.py
@@ -10,7 +10,10 @@
 
 
 def reduce_amplitudes(kernel_part, own_rows, far_rows, weights, excitation):
-    kernel = lax.psum(kernel_part, "aux")
+    count, kernel = (lax.axis_size("aux"), kernel_part)
+    for far in [1 << k for k in range(count.bit_length() - 1)]:
+        swap = [(i, i ^ far) for i in range(count)]
+        kernel = kernel + lax.ppermute(kernel, "aux", swap)
     return amplitudes(kernel, own_rows, far_rows, weights, excitation)
 
 

time: 210 us -> 248 us (1.18)
  waiting for transfers between devices: 84.2 us -> 133 us
  between operations: 13.4 us -> 0.05 us
  starting transfers between devices: 0.01 us -> 4.17 us
    ppermute x0 -> x2, waiting for transfers between devices: none -> 133 us  [reduce_amplitudes(): kernel = kernel + lax.ppermute(kernel, 'aux', swap)]
    psum x1 -> x0, waiting for transfers between devices: 84.2 us -> none  [reduce_amplitudes(): kernel = lax.psum(kernel_part, 'aux')]
    ppermute x0 -> x2, starting transfers between devices: none -> 4.17 us  [reduce_amplitudes(): kernel = kernel + lax.ppermute(kernel, 'aux', swap)]
  transfers between devices with their start and end apart: 1 -> 2, of which waited for: 1 -> 2; matrix products, arithmetic and copies ran while one was open for 1% -> 1% of each run, Pallas kernels for 0% -> 0%
where the time goes in v1:
time: 248 us
  waiting for transfers between devices  133 us (54%)
  blocking collectives  76.5 us (31%)
  matrix products  18.9 us (8%)
  local copies, waits for them, and re-layouts  8.98 us (4%)
  other arithmetic  6.52 us (3%)
  starting transfers between devices  4.17 us (2%)
    ppermute x2, waiting for transfers between devices, reduce_amplitudes(): kernel = kernel + lax.ppermute(kernel, 'aux', swap)  133 us
    all_to_all x1, blocking collectives, on_device(): lax.all_to_all(outgoing, 'orb', split_axis=0, concat_axis=0, tiled=True)  76.5 us
    dot_general x1, matrix products, accumulate(): jnp.einsum('si,sap->iap', pieces[2], product, precision=lax.Precision.HIG...  11.2 us
    dot_general x1, matrix products, accumulate(): jnp.einsum('sab,sbp->sap', pieces[0], pieces[1], preferred_element_type=j...  5.91 us
  transfers between devices with their start and end apart: 2, of which 2 were waited for; matrix products, arithmetic and copies ran while one was open for 1% of the time, Pallas kernels for 0%

profile of v1, /device:TPU:0, one launch (start us, length us, event | category | flops | bytes accessed | tf_op | source)
XLA Modules:
  0.0 247.8 jit_solution(17168872518858006059)
XLA Ops:
  0.0 0.0 copy-start
  0.0 0.9 constant_dynamic-slice_fusion.2
  0.9 0.1 copy.8
  1.0 0.7 fusion.17
  1.7 0.2 copy-done
  1.9 3.6 %gather_fusion = bf16[8,256,1536]{2,1,0:T(8,128)(2,1)} fusion(bf16[4,256,1536]{2,1,0:T(8,128)(2,1)S(1)} %copy-done, s32[1024]{0:T(1024)S(1)} %pad_clamp_fusion.2), kind=kCustom, calls=%fused_computation | custom fusion | bytes 12582944 | tf_op jit(solution)/shard_map/jit(_take)/gather | solution.py:30
  5.5 3.5 %broadcast_select_fusion = bf16[8,256,1536]{2,1,0:T(8,128)(2,1)S(1)} fusion(bf16[8,256,1536]{2,1,0:T(8,128)(2,1)} %gather_fusion, pred[8]{0:T(512)(128)(4,1)S(1)} %and_bitcast_fusion), kind=kLoop, calls=%fused_computation.5 | loop fusion | flops 3145728 | bytes 12582920 | tf_op jit(solution)/shard_map/jit(_take)/select_n | solution.py:30
  9.0 76.5 %all_to_all.5 = bf16[8,256,1536]{2,1,0:T(8,128)(2,1)S(1)} all-to-all(bf16[8,256,1536]{2,1,0:T(8,128)(2,1)S(1)} %broadcast_select_fusion), channel_id=1, replica_groups=mesh['orb'=8,'aux'=4] {'orb'}, dimensions={0} | all-to-all | bytes 12582912 | tf_op jit(solution)/shard_map/all_to_all | solution.py:31
  85.5 0.0 copy-start.1
  85.5 1.8 fusion.20
  87.3 0.8 copy-done.1
  88.1 0.0 copy-start.2
  88.1 1.6 collective-permute-start
  89.7 45.1 %collective-permute-done = f32[8,256,256]{2,1,0:T(8,128)S(1)} collective-permute-done((f32[8,256,256]{2,1,0:T(8,128)S(1)}, f32[8,256,256]{2,1,0:T(8,128)S(1)}, u32[]{:S(2)}, u32[]{:S(2)}) %collective-permute-start) | collective-permute-done | bytes 2097184 | tf_op jit(solution)/shard_map/ppermute | solution.py:16
  134.8 1.7 add.67
  136.5 2.6 %collective-permute-start.1 = (f32[8,256,256]{2,1,0:T(8,128)}, f32[8,256,256]{2,1,0:T(8,128)}, u32[]{:S(2)}, u32[]{:S(2)}) collective-permute-start(f32[8,256,256]{2,1,0:T(8,128)} %add.67), channel_id=1, source_target_pairs={{0,2},{1,3},{2,0},{3,1},{4,6},{5,7},{6,4},{7,5},{8,10},{9,11},{10,... | collective-permute-start | bytes 6291464 | tf_op jit(solution)/shard_map/ppermute | solution.py:16
  139.1 0.0 copy-done.2
  139.1 0.6 gather_fusion.1
  139.7 0.6 gather_fusion.2
  140.2 0.7 fusion.14
  140.9 87.5 %collective-permute-done.1 = f32[8,256,256]{2,1,0:T(8,128)} collective-permute-done((f32[8,256,256]{2,1,0:T(8,128)}, f32[8,256,256]{2,1,0:T(8,128)}, u32[]{:S(2)}, u32[]{:S(2)}) %collective-permute-start.1) | collective-permute-done | bytes 2097184 | tf_op jit(solution)/shard_map/ppermute | solution.py:16
  228.4 5.9 %fusion.5 = f32[8,256,1536]{2,1,0:T(8,128)S(1)} fusion(bf16[8,256,1536]{2,1,0:T(8,128)(2,1)} %copy-done.1, f32[8,256,256]{2,1,0:T(8,128)} %add.67, f32[8,256,256]{2,1,0:T(8,128)} %collective-permute-done.1, f32[8,256]{1,0:T(8,128)S(1)} %gather_fusion.2, f32[8,256]{1,0:T(8,128)S(1)} %gather_fusion.1, f32[8]{0:T(128)S(1)} %fusion.14), kind=kOutput, calls=%fused_computation.8 | convolution fusion | flops 1613234176 | bytes 23085088 | tf_op jit(solution)/shard_map/while/body/eval_jaxpr/sab,sbp->sap/dot_general | solution.py:44
  234.4 11.2 %fusion.2 = bf16[4,256,1536]{2,0,1:T(4,128)(2,1)S(1)} fusion(f32[8,256,1536]{2,1,0:T(8,128)S(1)} %fusion.5, s32[8]{0:T(128)S(1)} %bitcast.25), kind=kOutput, calls=%fused_computation.6 | convolution fusion | flops 152567840 | bytes 15728672 | tf_op jit(solution)/shard_map/while/body/eval_jaxpr/si,sap->iap/dot_general | solution.py:47
  245.6 2.2 copy.6
  (4 shorter events, 0.0 us)
Async XLA Ops:
  0.0 1.9 copy-start
  85.5 2.6 %copy-start.1 = (bf16[8,256,1536]{2,1,0:T(8,128)(2,1)}, bf16[8,256,1536]{2,1,0:T(8,128)(2,1)S(1)}, u32[]{:S(2)}) copy-start(bf16[8,256,1536]{2,1,0:T(8,128)(2,1)S(1)} %all_to_all.5) | copy-start | bytes 18874372
  88.1 51.0 %copy-start.2 = (f32[32,256]{1,0:T(8,128)S(1)}, f32[32,256]{1,0:T(8,128)}, u32[]{:S(2)}) copy-start(f32[32,256]{1,0:T(8,128)} %param.5) | copy-start | bytes 98308
  88.1 46.7 %collective-permute-start = (f32[8,256,256]{2,1,0:T(8,128)S(1)}, f32[8,256,256]{2,1,0:T(8,128)S(1)}, u32[]{:S(2)}, u32[]{:S(2)}) collective-permute-start(f32[8,256,256]{2,1,0:T(8,128)S(1)} %fusion.20), channel_id=1, source_target_pairs={{0,1},{1,0},{2,3},{3,2},{4,5},{5,4},{6,7},{7,6},{8,9},{9,8},{10,11... | collective-permute-start | bytes 6291464 | tf_op jit(solution)/shard_map/ppermute | solution.py:16
  136.5 92.0 %collective-permute-start.1 = (f32[8,256,256]{2,1,0:T(8,128)}, f32[8,256,256]{2,1,0:T(8,128)}, u32[]{:S(2)}, u32[]{:S(2)}) collective-permute-start(f32[8,256,256]{2,1,0:T(8,128)} %add.67), channel_id=1, source_target_pairs={{0,2},{1,3},{2,0},{3,1},{4,6},{5,7},{6,4},{7,5},{8,10},{9,11},{10,... | collective-permute-start | bytes 6291464 | tf_op jit(solution)/shard_map/ppermute | solution.py:16
